TPU v7x, 32 devices: a whole 2x2x4 slice. The times are simulated.
32 devices in a mesh: groups: 2 (over y), freq: 16 (over z, x, core).
Axes of the slice: x: 2, y: 2, z: 4, core: 2. Of those that a mesh axis runs over, the one named last changes fastest.
Arguments:
- refl: bfloat16 [128, 2, 512, 512], P(('groups', 'freq')), parts along dimension 0, may hold values from -0.1875 to 0.1875
- refl_scale: float32 [128, 4], P(('groups', 'freq')), parts along dimension 0, may hold values from 0.5 to 4
- freq_index: int32 [128], P(('groups', 'freq')), parts along dimension 0, may hold values from 1 to 1023, as said below
- fd_plus: bfloat16 [4096, 32, 512], P(('groups', 'freq')), parts along dimension 0, may hold values from -6 to 6
- onset: int32 [32768], P(('groups', 'freq')), parts along dimension 0, may hold values from 128 to 767
Outputs:
- f_minus: bfloat16 [4096, 32, 512], P(('groups', 'freq')), parts along dimension 0
- f_plus: float32 [4096, 32, 512], P(('groups', 'freq')), parts along dimension 0
There are 2 independent parts, one for each index of `groups`. A program takes and returns all parts, laid end to end along the dimension named above; each array names one. Nothing has to cross between parts.
Inputs may be any that keep to these rules, and one draw needn't show every extreme that they name: `freq_index`: the bins are distinct and ascending; the first is 1 and the last is 1023.
All inputs are finite; a program needn't handle non-finite values.
Results may differ from a plain program's by a relative error of at most 0.01.
Values may be sent and summed in bfloat16 or wider, within the bound.
No kernel may reach another device: no remote copies, remote signals or barrier semaphores. Data moves between devices by JAX's collectives and lax.ppermute only.
A program may use at most 128 MiB of HBM per device.

v0:
```python
import math
import jax
import jax.numpy as jnp
from jax import lax
from jax.sharding import PartitionSpec as P


def to_columns(field):
    return lax.all_to_all(field, "freq", split_axis=1, concat_axis=0, tiled=True)


def to_time(field):
    return lax.all_to_all(field, "freq", split_axis=0, concat_axis=1, tiled=True)


def local(refl, refl_scale, freq_index, fd_plus, onset):
    nfreq_dev = refl.shape[0]
    nrec = refl.shape[2]
    t_dev, points, _ = fd_plus.shape
    columns = points * nrec
    nshard = lax.axis_size("freq")
    ntime = t_dev * nshard
    width = columns // nshard
    first_col = lax.axis_index("freq") * width
    bins, scales = (
        lax.all_gather(freq_index, "freq", axis=0, tiled=True),
        lax.all_gather(refl_scale, "freq", axis=0, tiled=True),
    )
    nblocks = scales.shape[1]
    times = jnp.arange(ntime, dtype=jnp.int32)
    phase = bins[:, None] * times[None, :] % ntime
    angle = phase.astype(jnp.float32) * jnp.float32(2.0 * math.pi / ntime)
    cosine = jnp.cos(angle).astype(jnp.bfloat16)
    sine = jnp.sin(angle).astype(jnp.bfloat16)
    col_ids = first_col + jnp.arange(width, dtype=jnp.int32)
    block_ids = col_ids % nrec // (nrec // nblocks)
    onehot = (block_ids[None, :] == jnp.arange(nblocks, dtype=jnp.int32)[:, None]).astype(
        jnp.float32
    )
    col_scale = jnp.dot(
        scales, onehot, precision=lax.Precision.HIGHEST, preferred_element_type=jnp.float32
    )
    signed = jnp.where(times < ntime // 2, times, times - ntime)
    keep = (jnp.abs(signed)[:, None] < onset[None, :]).astype(jnp.float32)
    contract_time = (((0,), (0,)), ((), ()))

    def forward(colfield, table_c, table_s):
        real = jnp.dot(table_c, colfield, preferred_element_type=jnp.float32)
        imag = -jnp.dot(table_s, colfield, preferred_element_type=jnp.float32)
        spectrum = jnp.stack(
            [(real * col_scale).astype(jnp.bfloat16), (imag * col_scale).astype(jnp.bfloat16)],
            axis=1,
        )
        return lax.all_to_all(spectrum, "freq", split_axis=0, concat_axis=2, tiled=True)

    def convolve(spectrum, sign):
        spectrum = spectrum.reshape(nfreq_dev, 2, points, nrec)
        spec_r = spectrum[:, 0]
        spec_i = spectrum[:, 1]
        resp_r = refl[:, 0]
        resp_i = refl[:, 1]

        def apply(resp, spec):
            return jnp.einsum("frs,fvs->fvr", resp, spec, preferred_element_type=jnp.float32)

        out_r = apply(resp_r, spec_r) - sign * apply(resp_i, spec_i)
        out_i = apply(resp_r, spec_i) + sign * apply(resp_i, spec_r)
        stacked = jnp.stack([out_r.astype(jnp.bfloat16), out_i.astype(jnp.bfloat16)], axis=1)
        return lax.all_to_all(
            stacked.reshape(nfreq_dev, 2, columns), "freq", split_axis=2, concat_axis=0, tiled=True
        )

    def inverse(spectrum):
        trace = lax.dot_general(
            cosine, spectrum[:, 0], contract_time, preferred_element_type=jnp.float32
        )
        trace = trace - lax.dot_general(
            sine, spectrum[:, 1], contract_time, preferred_element_type=jnp.float32
        )
        return (trace * jnp.float32(2.0 / ntime) * keep).astype(jnp.bfloat16)

    direct = fd_plus.reshape(t_dev, columns)
    minus_cols = inverse(convolve(forward(to_columns(direct), cosine, sine), 1.0))
    minus_time = to_time(minus_cols)
    update_cols = inverse(convolve(forward(minus_cols, cosine, sine), -1.0))
    plus_time = direct.astype(jnp.float32) + to_time(update_cols).astype(jnp.float32)
    return (minus_time.reshape(t_dev, points, nrec), plus_time.reshape(t_dev, points, nrec))


def solution(mesh):
    return jax.shard_map(
        local,
        mesh=mesh,
        in_specs=(
            P(("groups", "freq"), None, None, None),
            P(("groups", "freq"), None),
            P(("groups", "freq")),
            P(("groups", "freq"), None, None),
            P(("groups", "freq")),
        ),
        out_specs=(P(("groups", "freq"), None, None), P(("groups", "freq"), None, None)),
        check_vma=False,
    )
```

profile of v0, /device:TPU:11, one launch (start us, length us, event | category | flops | bytes accessed | tf_op | source)
XLA Modules:
  0.0 541.2 jit_solution(8030469073627968279)
XLA Ops:
  0.6 7.9 %copy.51 = bf16[128,32,512]{0,2,1:T(8,128)(2,1)} copy(bf16[128,32,512]{2,1,0:T(8,128)(2,1)} %param.8) | data formatting | bytes 8388608 | tf_op args[3]
  8.5 6.7 %all-to-all-start = ((bf16[128,16,1024]{0,2,1:T(8,128)(2,1)}), bf16[128,16,1024]{0,2,1:T(8,128)(2,1)}, u32[]{:S(2)}, u32[]{:S(2)}) async-start(bf16[128,16,1024]{0,2,1:T(8,128)(2,1)} %bitcast.126), calls=%async_computation | async-start | bytes 8388608 | tf_op jit(solution)/shard_map/all_to_all | solution.py:9
  16.7 88.9 %all-reduce = s32[64]{0:T(128)S(1)} all-reduce(s32[64]{0:T(128)S(1)} %dynamic-update-slice), channel_id=1, replica_groups=mesh['groups'=2,'freq'=16] {'freq'}, use_global_device_ids=true, to_apply=%add | all-reduce | flops 64 | bytes 512
  105.6 18.6 %all-gather = f32[16,4,4]{2,1,0:T(4,128)S(1)} all-gather(f32[1,4,4]{2,1,0:T(4,128)S(1)} %bitcast.140), channel_id=1, replica_groups=mesh['groups'=2,'freq'=16] {'freq'}, dimensions={0}, use_global_device_ids=true | all-gather | bytes 1088 | tf_op jit(solution)/shard_map/all_gather | solution.py:27
  124.5 6.4 %copy.52 = bf16[16,128,1024]{2,1,0:T(8,128)(2,1)} copy(bf16[16,128,1024]{1,2,0:T(8,128)(2,1)} %bitcast.2) | data formatting | bytes 8388608 | tf_op jit(solution)/shard_map/all_to_all | solution.py:9
  130.9 4.5 fusion.64
  138.2 15.2 %all_to_all.114 = bf16[64,2,1024]{2,1,0:T(2,128)(2,1)S(1)} all-to-all(bf16[64,2,1024]{2,1,0:T(2,128)(2,1)S(1)} %copy.53), channel_id=1, replica_groups=mesh['groups'=2,'freq'=16] {'freq'}, dimensions={0} | all-to-all | bytes 524288 | tf_op jit(solution)/shard_map/all_to_all | solution.py:54
  161.9 13.0 %copy.57 = bf16[4,2,16384]{0,1,2:T(2,128)(2,1)} copy(bf16[4,2,16384]{2,0,1:T(4,128)(2,1)S(1)} %pad_maximum_fusion.1) | data formatting | bytes 524288 | tf_op jit(solution)/shard_map/stack | solution.py:68
  174.9 16.8 %reshape.93 = bf16[16,2,4096]{2,1,0:T(2,128)(2,1)} reshape(bf16[16384,2,4]{2,1,0:T(2,128)(2,1)} %bitcast.122) | data formatting | bytes 524288
  191.7 6.1 %all-to-all-start.2 = ((bf16[16,2,4096]{2,1,0:T(2,128)(2,1)}), bf16[16,2,4096]{2,1,0:T(2,128)(2,1)S(1)}, u32[]{:S(2)}, u32[]{:S(2)}) async-start(bf16[16,2,4096]{2,1,0:T(2,128)(2,1)} %reshape.93), calls=%async_computation.2 | async-start | bytes 524288 | tf_op jit(solution)/shard_map/all_to_all | solution.py:69
  197.8 7.9 %all-to-all-done.2 = bf16[16,2,4096]{2,1,0:T(2,128)(2,1)S(1)} async-done(((bf16[16,2,4096]{2,1,0:T(2,128)(2,1)}), bf16[16,2,4096]{2,1,0:T(2,128)(2,1)S(1)}, u32[]{:S(2)}, u32[]{:S(2)}) %all-to-all-start.2) | async-done | bytes 262176 | tf_op jit(solution)/shard_map/all_to_all | solution.py:69
  205.7 19.0 %reshape.94 = bf16[16384,2,4]{2,1,0:T(2,128)(2,1)} reshape(bf16[16,2,4096]{2,1,0:T(2,128)(2,1)S(1)} %all-to-all-done.2) | data formatting | bytes 524288
  224.7 11.9 %copy.67 = bf16[4,2,16,1024]{3,2,1,0:T(8,128)(2,1)S(1)} copy(bf16[4,2,16,1024]{0,1,3,2:T(2,128)(2,1)} %bitcast.123) | data formatting | bytes 524288 | tf_op jit(solution)/shard_map/all_to_all | solution.py:69
  240.4 4.1 fusion
  249.9 13.0 %all_to_all.115 = bf16[64,2,1024]{2,1,0:T(2,128)(2,1)S(1)} all-to-all(bf16[64,2,1024]{2,1,0:T(2,128)(2,1)S(1)} %copy.61), channel_id=1, replica_groups=mesh['groups'=2,'freq'=16] {'freq'}, dimensions={0} | all-to-all | bytes 524288 | tf_op jit(solution)/shard_map/all_to_all | solution.py:54
  271.4 13.0 %copy.63 = bf16[4,2,16384]{0,1,2:T(2,128)(2,1)} copy(bf16[4,2,16384]{2,0,1:T(4,128)(2,1)S(1)} %pad_maximum_fusion.3) | data formatting | bytes 524288 | tf_op jit(solution)/shard_map/stack | solution.py:68
  284.4 16.2 %reshape.95 = bf16[16,2,4096]{2,1,0:T(2,128)(2,1)S(1)} reshape(bf16[16384,2,4]{2,1,0:T(2,128)(2,1)} %bitcast.124) | data formatting | bytes 524288
  300.6 12.8 %all_to_all.116 = bf16[16,2,4096]{2,1,0:T(2,128)(2,1)S(1)} all-to-all(bf16[16,2,4096]{2,1,0:T(2,128)(2,1)S(1)} %reshape.95), channel_id=1, replica_groups=mesh['groups'=2,'freq'=16] {'freq'}, dimensions={0} | all-to-all | bytes 524288 | tf_op jit(solution)/shard_map/all_to_all | solution.py:69
  313.4 6.5 %all-to-all-start.3 = ((bf16[16,128,1024]{2,1,0:T(8,128)(2,1)}), bf16[16,128,1024]{2,1,0:T(8,128)(2,1)}, u32[]{:S(2)}, u32[]{:S(2)}) async-start(bf16[16,128,1024]{2,1,0:T(8,128)(2,1)} %bitcast.127), calls=%async_computation.3 | async-start | bytes 8388608 | tf_op jit(solution)/shard_map/all_to_all | solution.py:13
  319.9 19.1 %reshape.96 = bf16[16384,2,4]{2,1,0:T(2,128)(2,1)} reshape(bf16[16,2,4096]{2,1,0:T(2,128)(2,1)S(1)} %all_to_all.116) | data formatting | bytes 524288
  338.9 11.9 %copy.68 = bf16[4,2,16,1024]{3,2,1,0:T(8,128)(2,1)S(1)} copy(bf16[4,2,16,1024]{0,1,3,2:T(2,128)(2,1)} %bitcast.125) | data formatting | bytes 524288 | tf_op jit(solution)/shard_map/all_to_all | solution.py:69
  351.5 3.1 fusion.72
  354.6 4.9 fusion.1
  359.5 52.8 %all-to-all-done.3 = bf16[16,128,1024]{2,1,0:T(8,128)(2,1)} async-done(((bf16[16,128,1024]{2,1,0:T(8,128)(2,1)}), bf16[16,128,1024]{2,1,0:T(8,128)(2,1)}, u32[]{:S(2)}, u32[]{:S(2)}) %all-to-all-start.3) | async-done | bytes 4194336 | tf_op jit(solution)/shard_map/all_to_all | solution.py:13
  412.4 5.2 all-to-all-start.6
  417.6 6.5 %copy.60 = bf16[128,16,1024]{2,1,0:T(8,128)(2,1)} copy(bf16[128,16,1024]{2,0,1:T(8,128)(2,1)} %bitcast.19) | data formatting | bytes 8388608 | tf_op jit(solution)/shard_map/all_to_all | solution.py:13
  424.1 7.1 %reshape.83 = bf16[128,32,512]{2,1,0:T(8,128)(2,1)} reshape(bf16[128,16,1024]{2,1,0:T(8,128)(2,1)} %copy.60) | data formatting | bytes 8388608 | tf_op jit(solution)/shard_map/reshape | solution.py:87
  431.2 78.7 %all-to-all-done.6 = bf16[16,128,1024]{2,1,0:T(8,128)(2,1)} async-done(((bf16[16,128,1024]{2,1,0:T(8,128)(2,1)}), bf16[16,128,1024]{2,1,0:T(8,128)(2,1)}, u32[]{:S(2)}, u32[]{:S(2)}) %all-to-all-start.6) | async-done | bytes 4194336 | tf_op jit(solution)/shard_map/all_to_all | solution.py:13
  509.9 3.2 convert_bitcast_fusion
  513.2 8.3 %copy.66 = f32[128,16,1024]{2,1,0:T(8,128)} copy(f32[128,16,1024]{2,0,1:T(8,128)S(1)} %convert_bitcast_fusion) | data formatting | bytes 16777216 | tf_op jit(solution)/shard_map/convert_element_type | solution.py:86
  521.4 9.3 %reshape.85 = f32[128,32,512]{2,1,0:T(8,128)} reshape(f32[128,16,1024]{2,1,0:T(8,128)} %copy.66) | data formatting | bytes 16777216 | tf_op jit(solution)/shard_map/convert_element_type | solution.py:86
  530.7 10.2 %convert_add_fusion = f32[128,32,512]{2,1,0:T(8,128)} fusion(f32[128,32,512]{2,1,0:T(8,128)} %reshape.85, bf16[128,32,512]{2,1,0:T(8,128)(2,1)} %param.8), kind=kLoop, calls=%fused_computation.5 | loop fusion | flops 4194304 | bytes 20971520 | tf_op jit(solution)/shard_map/add | solution.py:86
  (53 shorter events, 30.4 us)
Async XLA Ops:
  8.5 6.7 %copy-start.7 = (u32[32]{0:T(128)S(1)}, u32[32]{0:T(128)}, u32[]{:S(2)}) copy-start(u32[32]{0:T(128)} %constant.68) | copy-start | bytes 388
  8.5 8.0 %copy-start.6 = (s32[4]{0:T(128)S(1)}, s32[4]{0:T(128)}, u32[]{:S(2)}) copy-start(s32[4]{0:T(128)} %param.7) | copy-start | bytes 52
  8.5 97.1 %copy-start.4 = (f32[4,4]{1,0:T(4,128)S(1)}, f32[4,4]{1,0:T(4,128)}, u32[]{:S(2)}) copy-start(f32[4,4]{1,0:T(4,128)} %param.6) | copy-start | bytes 196
  8.5 115.9 %all-to-all-start = ((bf16[128,16,1024]{0,2,1:T(8,128)(2,1)}), bf16[128,16,1024]{0,2,1:T(8,128)(2,1)}, u32[]{:S(2)}, u32[]{:S(2)}) async-start(bf16[128,16,1024]{0,2,1:T(8,128)(2,1)} %bitcast.126), calls=%async_computation | async-start | bytes 8388608 | tf_op jit(solution)/shard_map/all_to_all | solution.py:9
  130.9 4.5 copy-start.3
  153.7 4.8 copy-start
  191.7 14.0 %all-to-all-start.2 = ((bf16[16,2,4096]{2,1,0:T(2,128)(2,1)}), bf16[16,2,4096]{2,1,0:T(2,128)(2,1)S(1)}, u32[]{:S(2)}, u32[]{:S(2)}) async-start(bf16[16,2,4096]{2,1,0:T(2,128)(2,1)} %reshape.93), calls=%async_computation.2 | async-start | bytes 524288 | tf_op jit(solution)/shard_map/all_to_all | solution.py:69
  237.3 3.1 copy-start.5
  244.5 5.1 copy-start.2
  263.2 4.8 copy-start.1
  313.4 99.0 %all-to-all-start.3 = ((bf16[16,128,1024]{2,1,0:T(8,128)(2,1)}), bf16[16,128,1024]{2,1,0:T(8,128)(2,1)}, u32[]{:S(2)}, u32[]{:S(2)}) async-start(bf16[16,128,1024]{2,1,0:T(8,128)(2,1)} %bitcast.127), calls=%async_computation.3 | async-start | bytes 8388608 | tf_op jit(solution)/shard_map/all_to_all | solution.py:13
  412.4 97.6 %all-to-all-start.6 = ((bf16[16,128,1024]{2,1,0:T(8,128)(2,1)}), bf16[16,128,1024]{2,1,0:T(8,128)(2,1)}, u32[]{:S(2)}, u32[]{:S(2)}) async-start(bf16[16,128,1024]{2,1,0:T(8,128)(2,1)} %bitcast.128), calls=%async_computation.6 | async-start | bytes 8388608 | tf_op jit(solution)/shard_map/all_to_all | solution.py:13
where the time goes:
time: 550 us; the launch traced here: 541 us
  local copies, waits for them, and re-layouts  170 us (31%)
  blocking collectives  149 us (27%)
  waiting for transfers between devices  139 us (25%)
  matrix products  43.1 us (8%)
  starting transfers between devices  24.6 us (4%)
  other arithmetic  13.8 us (3%)
    all_to_all x2, waiting for transfers between devices, to_time(): lax.all_to_all(field, 'freq', split_axis=0, concat_axis=1, tiled=True)  132 us
    unnamed x1, blocking collectives  88.9 us
    unnamed x24, local copies, waits for them, and re-layouts  79.9 us
    all_to_all x2, blocking collectives, forward(): lax.all_to_all(spectrum, 'freq', split_axis=0, concat_axis=2, tiled=True)  28.2 us
    another operation x6, local copies, waits for them, and re-layouts, convolve(): jnp.stack([out_r.astype(jnp.bfloat16), out_i.astype(jnp.bfloat16)], axis=1)  26.2 us
    all_to_all x4, local copies, waits for them, and re-layouts, convolve(): lax.all_to_all(stacked.reshape(nfreq_dev, 2, columns), 'freq', split_axis...  24.3 us
    all_gather x1, blocking collectives, local(): lax.all_gather(refl_scale, 'freq', axis=0, tiled=True)  18.6 us
    convert_element_type x2, local copies, waits for them, and re-layouts, local(): to_time(update_cols).astype(jnp.float32)  17.6 us
  transfers between devices with their start and end apart: 4, of which 3 were waited for; matrix products, arithmetic and copies ran while one was open for 10% of the time, Pallas kernels for 0%

commit v1 on v0

--- a/solution.py
+++ b/solution.py
@@ -66,8 +66,16 @@
         out_r = apply(resp_r, spec_r) - sign * apply(resp_i, spec_i)
         out_i = apply(resp_r, spec_i) + sign * apply(resp_i, spec_r)
         stacked = jnp.stack([out_r.astype(jnp.bfloat16), out_i.astype(jnp.bfloat16)], axis=1)
-        return lax.all_to_all(
-            stacked.reshape(nfreq_dev, 2, columns), "freq", split_axis=2, concat_axis=0, tiled=True
+        return jnp.concatenate(
+            lax.all_to_all(
+                jnp.stack(
+                    jnp.split(stacked.reshape(nfreq_dev, 2, columns), lax.axis_size("freq"), axis=2)
+                ),
+                "freq",
+                0,
+                0,
+            ),
+            axis=0,
         )
 
     def inverse(spectrum):

time: 550 us -> 469 us (0.85)
  local copies, waits for them, and re-layouts: 170 us -> 48.4 us
  waiting for transfers between devices: 139 us -> 171 us
  other arithmetic: 13.8 us -> 24.6 us
    unnamed x24 -> x20, local copies, waits for them, and re-layouts: 79.9 us -> 8.75 us
    all_to_all x2, waiting for transfers between devices: 132 us -> 163 us  [to_time(): lax.all_to_all(field, 'freq', split_axis=0, concat_axis=1, tiled=True)]
    another operation x6 -> x4, local copies, waits for them, and re-layouts: 26.2 us -> 0.28 us  [convolve(): jnp.stack([out_r.astype(jnp.bfloat16), out_i.astype(jnp.bfloat16)], axis=1)]
    all_to_all x4 -> x0, local copies, waits for them, and re-layouts: 24.3 us -> none  [convolve(): lax.all_to_all(stacked.reshape(nfreq_dev, 2, columns), 'freq', split_axis...]
    unnamed x0 -> x30, other arithmetic: none -> 10.4 us
  transfers between devices with their start and end apart: 4 -> 4, of which waited for: 3 -> 3; matrix products, arithmetic and copies ran while one was open for 10% -> 5% of each run, Pallas kernels for 0% -> 0%
where the time goes in v1:
time: 469 us; the launch traced here: 462 us
  waiting for transfers between devices  171 us (36%)
  blocking collectives  149 us (32%)
  local copies, waits for them, and re-layouts  48.4 us (10%)
  matrix products  43.1 us (9%)
  starting transfers between devices  24.6 us (5%)
  other arithmetic  24.6 us (5%)
    all_to_all x2, waiting for transfers between devices, to_time(): lax.all_to_all(field, 'freq', split_axis=0, concat_axis=1, tiled=True)  163 us
    unnamed x1, blocking collectives  88.9 us
    all_to_all x2, blocking collectives, forward(): lax.all_to_all(spectrum, 'freq', split_axis=0, concat_axis=2, tiled=True)  28.2 us
    all_gather x1, blocking collectives, local(): lax.all_gather(refl_scale, 'freq', axis=0, tiled=True)  18.6 us
    convert_element_type x2, local copies, waits for them, and re-layouts, local(): to_time(update_cols).astype(jnp.float32)  17.6 us
    dot_general x8, matrix products, apply(): jnp.einsum('frs,fvs->fvr', resp, spec, preferred_element_type=jnp.float32)  15.6 us
    all_to_all x1, blocking collectives, convolve(): lax.all_to_all(jnp.stack(jnp.split(stacked.reshape(nfreq_dev, 2, columns)...  12.8 us
    all_to_all x2, starting transfers between devices, to_time(): lax.all_to_all(field, 'freq', split_axis=0, concat_axis=1, tiled=True)  11.7 us
  transfers between devices with their start and end apart: 4, of which 3 were waited for; matrix products, arithmetic and copies ran while one was open for 5% of the time, Pallas kernels for 0%

profile of v1, /device:TPU:11, one launch (start us, length us, event | category | flops | bytes accessed | tf_op | source)
XLA Modules:
  0.0 461.7 jit_solution(12148573190350197899)
XLA Ops:
  0.6 7.9 %copy.35 = bf16[128,32,512]{0,2,1:T(8,128)(2,1)} copy(bf16[128,32,512]{2,1,0:T(8,128)(2,1)} %param.8) | data formatting | bytes 8388608 | tf_op args[3]
  8.5 6.7 %all-to-all-start = ((bf16[128,16,1024]{0,2,1:T(8,128)(2,1)}), bf16[128,16,1024]{0,2,1:T(8,128)(2,1)}, u32[]{:S(2)}, u32[]{:S(2)}) async-start(bf16[128,16,1024]{0,2,1:T(8,128)(2,1)} %bitcast.242), calls=%async_computation | async-start | bytes 8388608 | tf_op jit(solution)/shard_map/all_to_all | solution.py:9
  16.7 88.9 %all-reduce = s32[64]{0:T(128)S(1)} all-reduce(s32[64]{0:T(128)S(1)} %dynamic-update-slice), channel_id=1, replica_groups=mesh['groups'=2,'freq'=16] {'freq'}, use_global_device_ids=true, to_apply=%add | all-reduce | flops 64 | bytes 512
  105.6 18.6 %all-gather = f32[16,4,4]{2,1,0:T(4,128)S(1)} all-gather(f32[1,4,4]{2,1,0:T(4,128)S(1)} %bitcast.254), channel_id=1, replica_groups=mesh['groups'=2,'freq'=16] {'freq'}, dimensions={0}, use_global_device_ids=true | all-gather | bytes 1088 | tf_op jit(solution)/shard_map/all_gather | solution.py:27
  124.5 6.4 %copy.36 = bf16[16,128,1024]{2,1,0:T(8,128)(2,1)} copy(bf16[16,128,1024]{1,2,0:T(8,128)(2,1)} %bitcast.2) | data formatting | bytes 8388608 | tf_op jit(solution)/shard_map/all_to_all | solution.py:9
  130.9 4.5 fusion.64
  135.4 2.5 fusion.65
  138.2 15.2 %all_to_all.88 = bf16[64,2,1024]{2,1,0:T(2,128)(2,1)S(1)} all-to-all(bf16[64,2,1024]{2,1,0:T(2,128)(2,1)S(1)} %copy.37), channel_id=1, replica_groups=mesh['groups'=2,'freq'=16] {'freq'}, dimensions={0} | all-to-all | bytes 524288 | tf_op jit(solution)/shard_map/all_to_all | solution.py:54
  153.7 2.4 fusion.6
  172.0 6.1 %all-to-all-start.2 = ((bf16[16,4,2,1024]{3,2,1,0:T(2,128)(2,1)}), bf16[16,4,2,1024]{3,2,1,0:T(2,128)(2,1)S(1)}, u32[]{:S(2)}, u32[]{:S(2)}) async-start(bf16[16,4,2,1024]{3,2,1,0:T(2,128)(2,1)} %constant_dynamic-update-slice_fusion), calls=%async_computation.2 | async-start | bytes 524288 | tf_op jit(solution)/shard_map/all_to_all | solution.py:70
  178.1 7.9 %all-to-all-done.2 = bf16[16,4,2,1024]{3,2,1,0:T(2,128)(2,1)S(1)} async-done(((bf16[16,4,2,1024]{3,2,1,0:T(2,128)(2,1)}), bf16[16,4,2,1024]{3,2,1,0:T(2,128)(2,1)S(1)}, u32[]{:S(2)}, u32[]{:S(2)}) %all-to-all-start.2) | async-done | bytes 262176 | tf_op jit(solution)/shard_map/all_to_all | solution.py:70
  186.4 3.1 fusion.73
  189.5 4.1 fusion
  193.6 2.5 fusion.62
  196.2 2.5 fusion.63
  199.0 13.0 %all_to_all.89 = bf16[64,2,1024]{2,1,0:T(2,128)(2,1)S(1)} all-to-all(bf16[64,2,1024]{2,1,0:T(2,128)(2,1)S(1)} %copy.44), channel_id=1, replica_groups=mesh['groups'=2,'freq'=16] {'freq'}, dimensions={0} | all-to-all | bytes 524288 | tf_op jit(solution)/shard_map/all_to_all | solution.py:54
  212.3 2.5 fusion.41
  214.8 2.3 fusion.38
  217.9 2.3 fusion.53
  221.2 12.8 %all_to_all.90 = bf16[16,4,2,1024]{3,2,1,0:T(2,128)(2,1)S(1)} all-to-all(bf16[16,4,2,1024]{3,2,1,0:T(2,128)(2,1)S(1)} %constant_dynamic-update-slice_fusion.16), channel_id=1, replica_groups=mesh['groups'=2,'freq'=16] {'freq'}, dimensions={0} | all-to-all | bytes 524288 | tf_op jit(solution)/shard_map/all_to_all | solution.py:70
  234.0 6.5 %all-to-all-start.3 = ((bf16[16,128,1024]{2,1,0:T(8,128)(2,1)}), bf16[16,128,1024]{2,1,0:T(8,128)(2,1)}, u32[]{:S(2)}, u32[]{:S(2)}) async-start(bf16[16,128,1024]{2,1,0:T(8,128)(2,1)} %bitcast.243), calls=%async_computation.3 | async-start | bytes 8388608 | tf_op jit(solution)/shard_map/all_to_all | solution.py:13
  240.8 3.1 fusion.72
  244.0 4.9 %fusion.1 = bf16[2048,1024]{1,0:T(8,128)(2,1)} fusion(f32[2048,1024]{1,0:T(8,128)S(1)} %fusion.72, s32[1024]{0:T(1024)S(1)} %copy-done.5, s32[2048]{0:T(1024)S(1)} %fusion.84, s32[64]{0:T(128)S(1)} %all-reduce, bf16[64,1,1024]{2,1,0:T(2,128)(2,1)S(1)} %get-tuple-element.2), kind=kOutput, calls=%fused_computation.3 | convolution fusion | flops 280887296 | bytes 12726528 | tf_op jit(solution)/shard_map/dot_general | solution.py:85
  248.9 84.1 %all-to-all-done.3 = bf16[16,128,1024]{2,1,0:T(8,128)(2,1)} async-done(((bf16[16,128,1024]{2,1,0:T(8,128)(2,1)}), bf16[16,128,1024]{2,1,0:T(8,128)(2,1)}, u32[]{:S(2)}, u32[]{:S(2)}) %all-to-all-start.3) | async-done | bytes 4194336 | tf_op jit(solution)/shard_map/all_to_all | solution.py:13
  332.9 5.2 %all-to-all-start.6 = ((bf16[16,128,1024]{2,1,0:T(8,128)(2,1)}), bf16[16,128,1024]{2,1,0:T(8,128)(2,1)}, u32[]{:S(2)}, u32[]{:S(2)}) async-start(bf16[16,128,1024]{2,1,0:T(8,128)(2,1)} %bitcast.244), calls=%async_computation.6 | async-start | bytes 8388608 | tf_op jit(solution)/shard_map/all_to_all | solution.py:13
  338.2 6.5 %copy.43 = bf16[128,16,1024]{2,1,0:T(8,128)(2,1)} copy(bf16[128,16,1024]{2,0,1:T(8,128)(2,1)} %bitcast.33) | data formatting | bytes 8388608 | tf_op jit(solution)/shard_map/all_to_all | solution.py:13
  344.7 7.1 %reshape.90 = bf16[128,32,512]{2,1,0:T(8,128)(2,1)} reshape(bf16[128,16,1024]{2,1,0:T(8,128)(2,1)} %copy.43) | data formatting | bytes 8388608 | tf_op jit(solution)/shard_map/reshape | solution.py:95
  351.8 78.7 %all-to-all-done.6 = bf16[16,128,1024]{2,1,0:T(8,128)(2,1)} async-done(((bf16[16,128,1024]{2,1,0:T(8,128)(2,1)}), bf16[16,128,1024]{2,1,0:T(8,128)(2,1)}, u32[]{:S(2)}, u32[]{:S(2)}) %all-to-all-start.6) | async-done | bytes 4194336 | tf_op jit(solution)/shard_map/all_to_all | solution.py:13
  430.5 3.2 convert_bitcast_fusion
  433.7 8.3 %copy.48 = f32[128,16,1024]{2,1,0:T(8,128)} copy(f32[128,16,1024]{2,0,1:T(8,128)S(1)} %convert_bitcast_fusion) | data formatting | bytes 16777216 | tf_op jit(solution)/shard_map/convert_element_type | solution.py:94
  442.0 9.3 %reshape.93 = f32[128,32,512]{2,1,0:T(8,128)} reshape(f32[128,16,1024]{2,1,0:T(8,128)} %copy.48) | data formatting | bytes 16777216 | tf_op jit(solution)/shard_map/convert_element_type | solution.py:94
  451.3 10.2 %convert_add_fusion = f32[128,32,512]{2,1,0:T(8,128)} fusion(f32[128,32,512]{2,1,0:T(8,128)} %reshape.93, bf16[128,32,512]{2,1,0:T(8,128)(2,1)} %param.8), kind=kLoop, calls=%fused_computation.5 | loop fusion | flops 4194304 | bytes 20971520 | tf_op jit(solution)/shard_map/add | solution.py:94
  (73 shorter events, 20.4 us)
Async XLA Ops:
  8.5 6.7 %copy-start.7 = (u32[32]{0:T(128)S(1)}, u32[32]{0:T(128)}, u32[]{:S(2)}) copy-start(u32[32]{0:T(128)} %constant.68) | copy-start | bytes 388
  8.5 8.0 %copy-start.6 = (s32[4]{0:T(128)S(1)}, s32[4]{0:T(128)}, u32[]{:S(2)}) copy-start(s32[4]{0:T(128)} %param.7) | copy-start | bytes 52
  8.5 97.1 %copy-start.4 = (f32[4,4]{1,0:T(4,128)S(1)}, f32[4,4]{1,0:T(4,128)}, u32[]{:S(2)}) copy-start(f32[4,4]{1,0:T(4,128)} %param.6) | copy-start | bytes 196
  8.5 115.9 %all-to-all-start = ((bf16[128,16,1024]{0,2,1:T(8,128)(2,1)}), bf16[128,16,1024]{0,2,1:T(8,128)(2,1)}, u32[]{:S(2)}, u32[]{:S(2)}) async-start(bf16[128,16,1024]{0,2,1:T(8,128)(2,1)} %bitcast.242), calls=%async_computation | async-start | bytes 8388608 | tf_op jit(solution)/shard_map/all_to_all | solution.py:9
  130.9 4.5 copy-start.3
  153.7 4.8 %copy-start = (bf16[4,2,512,512]{3,2,1,0:T(8,128)(2,1)S(1)}, bf16[4,2,512,512]{3,2,1,0:T(8,128)(2,1)}, u32[]{:S(2)}) copy-start(bf16[4,2,512,512]{3,2,1,0:T(8,128)(2,1)} %param.5) | copy-start | bytes 12582916
  172.0 14.0 %all-to-all-start.2 = ((bf16[16,4,2,1024]{3,2,1,0:T(2,128)(2,1)}), bf16[16,4,2,1024]{3,2,1,0:T(2,128)(2,1)S(1)}, u32[]{:S(2)}, u32[]{:S(2)}) async-start(bf16[16,4,2,1024]{3,2,1,0:T(2,128)(2,1)} %constant_dynamic-update-slice_fusion), calls=%async_computation.2 | async-start | bytes 524288 | tf_op jit(solution)/shard_map/all_to_all | solution.py:70
  186.4 3.1 copy-start.5
  193.6 5.1 %copy-start.2 = (bf16[2048,1024]{1,0:T(8,128)(2,1)}, bf16[2048,1024]{1,0:T(8,128)(2,1)S(1)}, u32[]{:S(2)}) copy-start(bf16[2048,1024]{1,0:T(8,128)(2,1)S(1)} %fusion) | copy-start | bytes 12582916
  212.3 4.8 %copy-start.1 = (bf16[4,2,512,512]{3,2,1,0:T(8,128)(2,1)S(1)}, bf16[4,2,512,512]{3,2,1,0:T(8,128)(2,1)}, u32[]{:S(2)}) copy-start(bf16[4,2,512,512]{3,2,1,0:T(8,128)(2,1)} %param.5) | copy-start | bytes 12582916
  234.0 99.0 %all-to-all-start.3 = ((bf16[16,128,1024]{2,1,0:T(8,128)(2,1)}), bf16[16,128,1024]{2,1,0:T(8,128)(2,1)}, u32[]{:S(2)}, u32[]{:S(2)}) async-start(bf16[16,128,1024]{2,1,0:T(8,128)(2,1)} %bitcast.243), calls=%async_computation.3 | async-start | bytes 8388608 | tf_op jit(solution)/shard_map/all_to_all | solution.py:13
  332.9 97.6 %all-to-all-start.6 = ((bf16[16,128,1024]{2,1,0:T(8,128)(2,1)}), bf16[16,128,1024]{2,1,0:T(8,128)(2,1)}, u32[]{:S(2)}, u32[]{:S(2)}) async-start(bf16[16,128,1024]{2,1,0:T(8,128)(2,1)} %bitcast.244), calls=%async_computation.6 | async-start | bytes 8388608 | tf_op jit(solution)/shard_map/all_to_all | solution.py:13
